TPU v7x, 32 devices: a whole 2x2x4 slice. The times are simulated.
32 devices in a mesh: dp: 8 (over y, x, core), tensor: 4 (over z).
Axes of the slice: x: 2, y: 2, z: 4, core: 2. Of those that a mesh axis runs over, the one named last changes fastest.
Arguments:
- inputs: bfloat16 [18432, 768], P('dp'), may hold values from -6 to 6
- cotangent: bfloat16 [18432, 768], P('dp'), may hold values from -6 to 6, as said below
- row_expert: int32 [18432], P('dp'), may hold values from 0 to 2, as said below
- row_keep: int32 [18432], P('dp'), may hold values from 0 to 1, as said below
- window_resolution: int32 [24], P('dp'), may hold values from 0 to 1, as said below
- attention_norm_gain: float32 [768], replicated, may hold values from 0.5 to 1.5
- attention_norm_bias: float32 [768], replicated, may hold values from -0.6 to 0.6
- qkv_weight: bfloat16 [3, 768, 768], P(None, None, 'tensor'), may hold values from -0.21875 to 0.21875
- qv_bias: float32 [2, 12, 64], P(None, 'tensor'), may hold values from -1.8 to 1.8
- out_weight: bfloat16 [768, 768], P('tensor'), may hold values from -2.5 to 2.5
- out_bias: float32 [768], replicated, may hold values from -0.6 to 0.6
- second_gain: float32 [3, 768], replicated, may hold values from 0.5 to 1.5
- expert_norm_bias: float32 [3, 768], replicated, may hold values from -0.6 to 0.6
- up_weight: bfloat16 [3, 768, 3072], P(None, None, 'tensor'), may hold values from -0.21875 to 0.21875
- up_bias: float32 [3, 3072], P(None, 'tensor'), may hold values from -0.6 to 0.6
- down_weight: bfloat16 [3, 3072, 768], P(None, 'tensor'), may hold values from -0.109375 to 0.109375
- down_bias: float32 [3, 768], replicated, may hold values from -0.6 to 0.6
Outputs:
- layer_out: bfloat16 [18432, 768], P('dp')
- input_rows_gradient: bfloat16 [18432, 768], P('dp')
- attention_gain_gradient: float32 [768], replicated
- grad_first_bias: float32 [768], replicated
- grad_qkv: float32 [3, 768, 768], P(None, 'dp', 'tensor')
- grad_qv_bias: float32 [2, 12, 64], P(None, 'tensor')
- grad_out_weight: float32 [768, 768], P('tensor', 'dp')
- grad_out_bias: float32 [768], replicated
- expert_gain_gradient: float32 [3, 768], replicated
- grad_second_bias: float32 [3, 768], replicated
- grad_up: float32 [3, 768, 3072], P(None, 'dp', 'tensor')
- grad_up_bias: float32 [3, 3072], P(None, 'tensor')
- grad_down: float32 [3, 3072, 768], P(None, 'tensor', 'dp')
- grad_down_bias: float32 [3, 768], replicated
Inputs may be any that keep to these rules, and one draw needn't show every extreme that they name: `row_expert`: rows come in windows of 768 slots. A window with window_resolution = 1 holds one pair: 577 image rows, then 1 to 64 text rows, then padding. One with 0 holds two pairs, one in each half of 384 slots, each of 197 image rows, then 1 to 64 text rows, then padding. In some pairs every real row uses expert 2; otherwise image rows use 0 and text rows 1. Padding rows use 1. `row_keep`: 1 on the image and text rows of a pair, 0 on its padding; every pair has padding and its first row is real. `window_resolution`: all windows of one index of dp have the same value. `cotangent`: 0 on every row with row_keep = 0.
All inputs are finite; a program needn't handle non-finite values.
Results may differ from a plain program's by a relative error of at most 0.015.
Values may be sent and summed in bfloat16 or wider, within the bound.
No kernel may reach another device: no remote copies, remote signals or barrier semaphores. Data moves between devices by JAX's collectives and lax.ppermute only.
A program may use at most 256 MiB of HBM per device.

v0:
```python
import math
import jax
import jax.numpy as jnp
from jax import lax
from jax.sharding import PartitionSpec as P

HEAD_DIM = 64
S = 768
BLK = 128
epsilon = 1e-05
masked_score = -1000000000.0


def gelu_exact(values):
    return jax.nn.gelu(values, approximate=False)


def apply_layer_norm(values):
    mean_row = jnp.mean(values, -1, keepdims=True)
    centred = values - mean_row
    variance = jnp.mean(centred * centred, -1, keepdims=True)
    inverse_deviation = lax.rsqrt(variance + epsilon)
    return (centred * inverse_deviation, inverse_deviation)


def norm_backward_pass(rowwise_gradient, centred_normalized, inverse_deviation, rowwise_gain):
    scaled_output = rowwise_gradient * rowwise_gain
    return inverse_deviation * (
        scaled_output
        - jnp.mean(scaled_output, -1, keepdims=True)
        - centred_normalized * jnp.mean(scaled_output * centred_normalized, -1, keepdims=True)
    )


def lookup_table_rows(table, expert_selector_float):
    result = jnp.zeros((expert_selector_float.shape[0], table.shape[1]), jnp.float32)
    for expert_id in range(table.shape[0]):
        result = (
            result + expert_selector_float[:, expert_id : expert_id + 1] * table[expert_id][None, :]
        )
    return result


def grouped_totals(expert_selector_float, values):
    return jnp.einsum("re,rd->ed", expert_selector_float, values, precision=lax.Precision.HIGHEST)


def total_rows(values):
    return lax.psum(values, "tensor")


def group_slots(onehot_int, row_count):
    expert_count = onehot_int.shape[1]
    counts = jnp.sum(onehot_int, 0)
    padded = (counts + BLK - 1) // BLK * BLK
    group_ends = jnp.cumsum(padded)
    group_starts = group_ends - padded
    row_ranks = jnp.cumsum(onehot_int, 0) - onehot_int
    row_slots = jnp.sum(onehot_int * (group_starts[None, :] + row_ranks), 1)
    block_count = row_count // BLK + expert_count - 1
    sources = jnp.full((block_count * BLK,), row_count, jnp.int32)
    sources = sources.at[row_slots].set(jnp.arange(row_count, dtype=jnp.int32))
    firsts = jnp.arange(block_count, dtype=jnp.int32) * BLK
    block_expert = jnp.minimum(
        jnp.sum((firsts[:, None] >= group_ends[None, :]).astype(jnp.int32), 1), expert_count - 1
    )
    return (row_slots, sources, block_expert)


def head_split(rows_in):
    return rows_in.reshape(rows_in.shape[0], rows_in.shape[1] // HEAD_DIM, HEAD_DIM)


def masked_scores(q_heads, k_heads, keep_rows, single):
    scale_factor = 1.0 / math.sqrt(HEAD_DIM)
    scores = (
        jnp.einsum("qhd,khd->hqk", q_heads, k_heads, preferred_element_type=jnp.float32)
        * scale_factor
    )
    positions = jnp.arange(keep_rows.shape[0], dtype=jnp.int32)
    upper = positions >= keep_rows.shape[0] // 2
    same_half = upper[:, None] == upper[None, :]
    allowed = (keep_rows[None, :] > 0) & (same_half | (single > 0))
    return jnp.where(allowed[None, :, :], scores, masked_score)


def attend_forward(pieces):
    query_rows, key_rows, value_rows, keep_rows, single = pieces
    q_heads, k_heads, v_heads = (
        head_split(query_rows),
        head_split(key_rows),
        head_split(value_rows),
    )
    scores = masked_scores(q_heads, k_heads, keep_rows, single)
    row_max = jnp.max(scores, -1, keepdims=True)
    exp_scores = jnp.exp(scores - row_max)
    exp_total = jnp.sum(exp_scores, -1, keepdims=True)
    weights = (exp_scores / exp_total).astype(jnp.bfloat16)
    log_totals = row_max[..., 0] + jnp.log(exp_total[..., 0])
    mixed_heads = jnp.einsum("hqk,khd->qhd", weights, v_heads, preferred_element_type=jnp.float32)
    return (mixed_heads.astype(jnp.bfloat16).reshape(query_rows.shape), log_totals)


def attend_backward(pieces):
    query_rows, key_rows, value_rows, keep_rows, single, log_totals, rowwise_gradient = pieces
    scale_factor = 1.0 / math.sqrt(HEAD_DIM)
    q_heads, k_heads, v_heads = (
        head_split(query_rows),
        head_split(key_rows),
        head_split(value_rows),
    )
    grad_heads = head_split(rowwise_gradient)
    scores = masked_scores(q_heads, k_heads, keep_rows, single)
    probs = jnp.exp(scores - log_totals[..., None])
    weights = probs.astype(jnp.bfloat16)
    grad_value = jnp.einsum("hqk,qhd->khd", weights, grad_heads, preferred_element_type=jnp.float32)
    grad_probs = jnp.einsum("qhd,khd->hqk", grad_heads, v_heads, preferred_element_type=jnp.float32)
    grad_scores = probs * (grad_probs - jnp.sum(probs * grad_probs, -1, keepdims=True))
    grad_scores = grad_scores.astype(jnp.bfloat16)
    grad_query = (
        jnp.einsum("hqk,khd->qhd", grad_scores, k_heads, preferred_element_type=jnp.float32)
        * scale_factor
    )
    grad_key = (
        jnp.einsum("hqk,qhd->khd", grad_scores, q_heads, preferred_element_type=jnp.float32)
        * scale_factor
    )
    return (
        grad_query.astype(jnp.bfloat16).reshape(query_rows.shape),
        grad_key.astype(jnp.bfloat16).reshape(query_rows.shape),
        grad_value.astype(jnp.bfloat16).reshape(query_rows.shape),
    )


def body(
    inputs,
    cotangent,
    row_expert,
    row_keep,
    window_resolution,
    attention_norm_gain,
    attention_norm_bias,
    qkv_weight,
    qv_bias,
    out_weight,
    out_bias,
    second_gain,
    expert_norm_bias,
    up_weight,
    up_bias,
    down_weight,
    down_bias,
):
    row_count, model_width = inputs.shape
    expert_count = up_weight.shape[0]
    local_width = qkv_weight.shape[2]
    seq_count = row_count // S
    share_count = row_count // lax.axis_size("tensor")
    share_start = lax.axis_index("tensor") * share_count

    def local_row_block(values):
        return lax.dynamic_slice_in_dim(values, share_start, share_count, 0)

    gathered_source_rows = inputs.astype(jnp.float32)
    onehot_int = (row_expert[:, None] == jnp.arange(expert_count, dtype=jnp.int32)[None, :]).astype(
        jnp.int32
    )
    expert_selector_float = onehot_int.astype(jnp.float32)
    expert_selector_local = local_row_block(expert_selector_float)
    attention_centred, attention_inverse_deviation = apply_layer_norm(gathered_source_rows)
    attention_normed = (attention_centred * attention_norm_gain + attention_norm_bias).astype(
        jnp.bfloat16
    )
    bias_pair = qv_bias.reshape(2, local_width)
    query = (
        jnp.dot(attention_normed, qkv_weight[0], preferred_element_type=jnp.float32) + bias_pair[0]
    ).astype(jnp.bfloat16)
    keyed = jnp.dot(attention_normed, qkv_weight[1], preferred_element_type=jnp.float32).astype(
        jnp.bfloat16
    )
    valued = (
        jnp.dot(attention_normed, qkv_weight[2], preferred_element_type=jnp.float32) + bias_pair[1]
    ).astype(jnp.bfloat16)
    seq_query = query.reshape(seq_count, S, local_width)
    seq_key = keyed.reshape(seq_count, S, local_width)
    seq_value = valued.reshape(seq_count, S, local_width)
    seq_keep = row_keep.reshape(seq_count, S)
    mixed_seq, log_totals = lax.map(
        attend_forward, (seq_query, seq_key, seq_value, seq_keep, window_resolution)
    )
    mixed = mixed_seq.reshape(row_count, local_width)
    attn_part = jnp.dot(mixed, out_weight, preferred_element_type=jnp.float32)
    residual_hidden = gathered_source_rows + (total_rows(attn_part) + out_bias)
    expert_centred, expert_inverse_deviation = apply_layer_norm(residual_hidden)
    rowwise_gain = lookup_table_rows(second_gain, expert_selector_float)
    expert_normed = (
        expert_centred * rowwise_gain + lookup_table_rows(expert_norm_bias, expert_selector_float)
    ).astype(jnp.bfloat16)
    expert_centred_local = local_row_block(expert_centred)
    row_slots, sources, block_expert = group_slots(onehot_int, row_count)
    block_count = block_expert.shape[0]
    zero_row = jnp.zeros((1, model_width), jnp.bfloat16)
    hidden_in = jnp.concatenate([expert_normed, zero_row], 0)[sources].reshape(
        block_count, BLK, model_width
    )

    def expert_block(pieces):
        block_in, expert_id = pieces
        up_mat = lax.dynamic_index_in_dim(up_weight, expert_id, 0, keepdims=False)
        down_mat = lax.dynamic_index_in_dim(down_weight, expert_id, 0, keepdims=False)
        up_row = lax.dynamic_index_in_dim(up_bias, expert_id, 0, keepdims=False)
        pre_act = jnp.dot(block_in, up_mat, preferred_element_type=jnp.float32) + up_row
        act_out = gelu_exact(pre_act).astype(jnp.bfloat16)
        block_out = jnp.dot(act_out, down_mat, preferred_element_type=jnp.float32)
        return (pre_act, act_out, block_out)

    pre_blocks, act_blocks, out_blocks = lax.map(expert_block, (hidden_in, block_expert))
    expert_part = out_blocks.reshape(block_count * BLK, model_width)[row_slots]
    layer_out = (
        residual_hidden
        + (total_rows(expert_part) + lookup_table_rows(down_bias, expert_selector_float))
    ).astype(jnp.bfloat16)
    cot_own = local_row_block(cotangent).astype(jnp.float32)
    grad_down_bias = grouped_totals(expert_selector_local, cot_own)
    grad_in_blocks = jnp.concatenate([cotangent, zero_row], 0)[sources].reshape(
        block_count, BLK, model_width
    )

    def expert_back(running, pieces):
        acc_up, acc_down, acc_up_bias = running
        block_in, pre_act, act_out, grad_block, expert_id = pieces
        up_mat = lax.dynamic_index_in_dim(up_weight, expert_id, 0, keepdims=False)
        down_mat = lax.dynamic_index_in_dim(down_weight, expert_id, 0, keepdims=False)
        grad_act = jnp.einsum("rd,fd->rf", grad_block, down_mat, preferred_element_type=jnp.float32)
        _, pullback = jax.vjp(gelu_exact, pre_act)
        grad_pre = pullback(grad_act)[0].astype(jnp.bfloat16)
        acc_up = acc_up.at[expert_id].add(
            jnp.einsum("rd,rf->df", block_in, grad_pre, preferred_element_type=jnp.float32)
        )
        acc_down = acc_down.at[expert_id].add(
            jnp.einsum("rf,rd->fd", act_out, grad_block, preferred_element_type=jnp.float32)
        )
        acc_up_bias = acc_up_bias.at[expert_id].add(jnp.sum(grad_pre.astype(jnp.float32), 0))
        grad_hidden = jnp.einsum("rf,df->rd", grad_pre, up_mat, preferred_element_type=jnp.float32)
        return ((acc_up, acc_down, acc_up_bias), grad_hidden)

    start_state = (
        jnp.zeros(up_weight.shape, jnp.float32),
        jnp.zeros(down_weight.shape, jnp.float32),
        jnp.zeros(up_bias.shape, jnp.float32),
    )
    (grad_up, grad_down, grad_up_bias), grad_hidden_blocks = lax.scan(
        expert_back, start_state, (hidden_in, pre_blocks, act_blocks, grad_in_blocks, block_expert)
    )
    hidden_part = grad_hidden_blocks.reshape(block_count * BLK, model_width)[row_slots]
    expert_normed_gradient = total_rows(hidden_part)
    residual_gradient = cotangent.astype(jnp.float32) + norm_backward_pass(
        expert_normed_gradient, expert_centred, expert_inverse_deviation, rowwise_gain
    )
    grad_attn = residual_gradient.astype(jnp.bfloat16)
    expert_normed_gradient_local = local_row_block(expert_normed_gradient)
    grad_attn_own = local_row_block(grad_attn)
    expert_gain_gradient = grouped_totals(
        expert_selector_local, expert_normed_gradient_local * expert_centred_local
    )
    grad_second_bias = grouped_totals(expert_selector_local, expert_normed_gradient_local)
    grad_out_bias = jnp.sum(grad_attn_own.astype(jnp.float32), 0)
    grad_out_weight = jnp.einsum("rh,rd->hd", mixed, grad_attn, preferred_element_type=jnp.float32)
    grad_mixed = jnp.einsum(
        "rd,hd->rh", grad_attn, out_weight, preferred_element_type=jnp.float32
    ).astype(jnp.bfloat16)
    grad_q_seq, grad_k_seq, grad_v_seq = lax.map(
        attend_backward,
        (
            seq_query,
            seq_key,
            seq_value,
            seq_keep,
            window_resolution,
            log_totals,
            grad_mixed.reshape(seq_count, S, local_width),
        ),
    )
    grad_query = grad_q_seq.reshape(row_count, local_width)
    grad_key = grad_k_seq.reshape(row_count, local_width)
    grad_value = grad_v_seq.reshape(row_count, local_width)
    grad_qkv = jnp.stack(
        [
            jnp.einsum("rd,rh->dh", attention_normed, grad_part, preferred_element_type=jnp.float32)
            for grad_part in (grad_query, grad_key, grad_value)
        ]
    )
    grad_qv_bias = jnp.stack(
        [jnp.sum(grad_query.astype(jnp.float32), 0), jnp.sum(grad_value.astype(jnp.float32), 0)]
    ).reshape(qv_bias.shape)
    first_part = jnp.einsum(
        "rh,dh->rd", grad_query, qkv_weight[0], preferred_element_type=jnp.float32
    )
    first_part = first_part + jnp.einsum(
        "rh,dh->rd", grad_key, qkv_weight[1], preferred_element_type=jnp.float32
    )
    first_part = first_part + jnp.einsum(
        "rh,dh->rd", grad_value, qkv_weight[2], preferred_element_type=jnp.float32
    )
    attention_centred_local = local_row_block(attention_centred)
    attention_normed_gradient = total_rows(first_part)
    input_rows_gradient = (
        residual_gradient
        + norm_backward_pass(
            attention_normed_gradient,
            attention_centred,
            attention_inverse_deviation,
            attention_norm_gain,
        )
    ).astype(jnp.bfloat16)
    attention_normed_gradient_local = local_row_block(attention_normed_gradient)
    attention_gain_gradient = jnp.sum(attention_normed_gradient_local * attention_centred_local, 0)
    grad_first_bias = jnp.sum(attention_normed_gradient_local, 0)
    summed_qkv, summed_out, summed_up, summed_down = (
        lax.psum_scatter(
            grad_qkv.astype(jnp.bfloat16), "dp", scatter_dimension=1, tiled=True
        ).astype(jnp.float32),
        lax.psum_scatter(
            grad_out_weight.astype(jnp.bfloat16), "dp", scatter_dimension=1, tiled=True
        ).astype(jnp.float32),
        lax.psum_scatter(
            grad_up.astype(jnp.bfloat16), "dp", scatter_dimension=1, tiled=True
        ).astype(jnp.float32),
        lax.psum_scatter(
            grad_down.astype(jnp.bfloat16), "dp", scatter_dimension=2, tiled=True
        ).astype(jnp.float32),
    )
    norm_sums = lax.psum(
        (
            attention_gain_gradient,
            grad_first_bias,
            grad_out_bias,
            expert_gain_gradient,
            grad_second_bias,
            grad_down_bias,
        ),
        ("dp", "tensor"),
    )
    small_sums = lax.psum((grad_qv_bias, grad_up_bias), "dp")
    return (
        layer_out,
        input_rows_gradient,
        norm_sums[0],
        norm_sums[1],
        summed_qkv,
        small_sums[0],
        summed_out,
        norm_sums[2],
        norm_sums[3],
        norm_sums[4],
        summed_up,
        small_sums[1],
        summed_down,
        norm_sums[5],
    )


def solution(mesh):
    in_specs = (
        P("dp", None),
        P("dp", None),
        P("dp"),
        P("dp"),
        P("dp"),
        P(),
        P(),
        P(None, None, "tensor"),
        P(None, "tensor", None),
        P("tensor", None),
        P(),
        P(),
        P(),
        P(None, None, "tensor"),
        P(None, "tensor"),
        P(None, "tensor", None),
        P(),
    )
    out_specs = (
        P("dp", None),
        P("dp", None),
        P(),
        P(),
        P(None, "dp", "tensor"),
        P(None, "tensor", None),
        P("tensor", "dp"),
        P(),
        P(),
        P(),
        P(None, "dp", "tensor"),
        P(None, "tensor"),
        P(None, "tensor", "dp"),
        P(),
    )
    return jax.shard_map(body, mesh=mesh, in_specs=in_specs, out_specs=out_specs, check_vma=False)
```

profile of v0, /device:TPU:0, one launch (start us, length us, event | category | flops | bytes accessed | tf_op | source)
XLA Modules:
  0.0 2110.5 jit_solution(14729037549028274431)
XLA Ops:
  13.2 5.3 fusion.82
  26.8 26.4 %while.59 = (s32[]{:T(128)}, bf16[3,768,192]{1,2,0:T(8,128)(2,1)}, f32[3,3,768]{2,1,0:T(4,128)}, bf16[3,768,192]{1,2,0:T(8,128)(2,1)S(1)}, s32[3,768]{1,0:T(4,12...) while((s32[]{:T(128)}, bf16[3,768,192]{1,2,0:T(8,128)(2,1)}, ...), condition=%wide.region_5.6_spmd, body=%wide.region_2.5_spmd.sunk | while | flops 476134656 | bytes 27215000 | solution.py:188
  66.1 9.0 scatter_custom_fusion
  75.1 13.0 gather_fusion.2
  89.1 222.3 %all-reduce.9.cloned.1.call-done = f32[2304,768]{1,0:T(8,128)} async-done(((f32[2304,768]{1,0:T(8,128)}), f32[2304,768]{1,0:T(8,128)}) %all-reduce.9.cloned.1.call-update) | async-done | bytes 7077904 | tf_op jit(solution)/shard_map/psum | solution.py:49
  311.3 5.2 fusion.127
  320.7 15.5 add_convert_fusion.2
  338.2 12.8 gather_fusion
  358.9 207.5 %while.60 = (s32[]{:T(128)}, f32[20,128,768]{2,1,0:T(8,128)}, bf16[20,128,768]{2,1,0:T(8,128)(2,1)}, f32[20,128,768]{2,1,0:T(8,128)}, bf16[20,128,768]{2,1,0:T(8...) while((s32[]{:T(128)}, f32[20,128,768]{2,1,0:T(8,128)}, ...), condition=%wide.region_17.18_spmd, body=%wide.region_16.17_spmd.sunk | while | flops 314867712 | bytes 4729531 | solution.py:217
  577.2 544.5 %while.61 = (s32[]{:T(128)}, f32[3,768,768]{2,1,0:T(8,128)}, f32[3,768,768]{1,2,0:T(8,128)}, f32[3,768]{1,0:T(4,128)S(1)}, f32[20,128,768]{2,1,0:T(8,128)}, /*in...) while((s32[]{:T(128)}, f32[3,768,768]{2,1,0:T(8,128)}, ...), condition=%wide.region_23.24_spmd, body=%wide.region_19.23_spmd.sunk | while | flops 613614336 | bytes 32857364 | solution.py:252
  860.9 4.3 fusion.210
  887.5 4.3 fusion.210
  914.2 4.3 fusion.210
  940.9 4.3 fusion.210
  967.5 4.3 fusion.210
  994.2 4.3 fusion.210
  1020.9 4.3 fusion.210
  1047.6 4.3 fusion.210
  1121.7 12.7 gather_fusion.3
  1134.4 5.6 convert_element_type.143
  1140.2 12.8 gather_fusion.1
  1153.0 5.4 convert_element_type.145
  1158.5 223.4 %all-reduce.11.cloned.1.call-done = f32[2304,768]{1,0:T(8,128)} async-done(((f32[2304,768]{1,0:T(8,128)}), f32[2304,768]{1,0:T(8,128)}) %all-reduce.11.cloned.1.call-update) | async-done | bytes 7077904 | tf_op jit(solution)/shard_map/psum | solution.py:49
  1381.8 8.2 fusion.128
  1390.5 8.0 fusion.129
  1401.3 51.2 %while.62 = (s32[]{:T(128)}, bf16[3,768,192]{1,2,0:T(8,128)(2,1)S(1)}, bf16[3,768,192]{1,2,0:T(8,128)(2,1)}, bf16[3,768,192]{1,2,0:T(8,128)(2,1)S(1)}, bf16[3,76...) while((s32[]{:T(128)}, ...), condition=%wide.region_29.30_spmd, body=%wide.region_27.29_spmd.sunk | while | flops 1161510144 | bytes 62592184 | solution.py:272
  1494.7 23.7 %all-reduce.3 = (f32[2,3,64]{2,1,0:T(4,128)S(1)}, f32[3,768]{1,0:T(4,128)}) all-reduce(f32[2,3,64]{2,1,0:T(4,128)S(1)} %pad_maximum_fusion.1, f32[3,768]{1,0:T(4,128)S(1)} %copy-done.23), channel_id=1, replica_groups=mesh['dp'=8,'tensor'=4] {'dp'}, use_global_device_ids=true, to_apply=%region_40.41 | all-reduce | flops 2688 | bytes 21504 | tf_op jit(solution)/shard_map/psum | solution.py:344
  1527.3 32.2 %reduce-scatter.13.cloned.1.call-done = bf16[96,576]{1,0:T(8,128)(2,1)} async-done(((bf16[768,576]{1,0:T(8,128)(2,1)}), bf16[96,576]{1,0:T(8,128)(2,1)}) %reduce-scatter.13.cloned.1.call-update) | async-done | bytes 110608
  1561.6 478.2 %all-reduce.13.cloned.1.call-done = (f32[2304,768]{1,0:T(8,128)}, f32[2304,768]{1,0:T(8,128)}) async-done(((f32[2304,768]{1,0:T(8,128)}, f32[2304,768]{1,0:T(8,128)}), (f32[2304,768]{1,0:T(8,128)}, f32[2304,768]{1,0:T(8,128)})) %all-reduce.13.cloned.1.call-update) | async-done | bytes 14155792 | tf_op jit(solution)/shard_map/psum | solution.py:49
  2039.8 5.5 multiply_reduce_fusion.4
  2047.6 40.5 %all-reduce.2 = (f32[768]{0:T(1024)}, f32[768]{0:T(1024)}, f32[768]{0:T(1024)}, f32[3,768]{1,0:T(4,128)}, f32[3,768]{1,0:T(4,128)}, /*index=5*/f32[3,768]{1,0:T(4,128)}) all-reduce(f32[768]{0:T(1024)S(1)} %get-tuple-element.415, f32[768]{0:T(1024)S(1)} %get-tuple-element.414, ...), channel_id=1, replica_groups=mesh['dp'=8,'tensor'=4] {'dp','tensor'}, use_global_device_ids=true, to_apply=%region_34.35 | all-reduce | flops 9216 | bytes 73728 | tf_op jit(solution)/shard_map/psum | solution.py:333
  2088.1 15.1 add_convert_fusion
  (626 shorter events, 811.9 us)
Async XLA Ops:
  7.2 48.9 %copy-start = (bf16[192,768]{1,0:T(8,128)(2,1)S(1)}, bf16[192,768]{1,0:T(8,128)(2,1)}, u32[]{:S(2)}) copy-start(bf16[192,768]{1,0:T(8,128)(2,1)} %param.40) | copy-start | bytes 884740
  7.2 5.9 copy-start.35
  7.2 6.0 copy-start.34
  7.2 6.0 copy-start.26
  7.2 304.1 %all-reduce.9.cloned.1.call-start = ((), (), s32[]{:S(2)}) async-start(), calls=%async_computation.4 | async-start | bytes 14155776 | tf_op jit(solution)/shard_map/psum | solution.py:49
  9.9 8.6 copy-start.14
  13.1 5.4 copy-start.18
  13.2 5.3 copy-start.12
  53.1 7.0 copy-start.4
  53.1 7.0 copy-start.5
  53.1 7.0 copy-start.6
  60.1 1321.7 %all-reduce.11.cloned.1.call-start = ((), (), s32[]{:S(2)}) async-start(), calls=%async_computation.5 | async-start | bytes 14155776 | tf_op jit(solution)/shard_map/psum | solution.py:49
  75.1 13.2 copy-start.31
  75.1 13.2 copy-start.32
  75.1 236.2 %copy-start.24 = (f32[768]{0:T(1024)S(1)}, f32[768]{0:T(1024)}, u32[]{:S(2)}) copy-start(f32[768]{0:T(1024)} %param.41) | copy-start | bytes 9220
  311.3 7.1 copy-start.2
  569.8 7.4 copy-start.28
  569.8 7.4 copy-start.29
  1121.7 12.7 copy-start.22
  1134.4 355.7 %reduce-scatter.9.cloned.1.call-start = ((), (), s32[]{:S(2)}) async-start(), calls=%async_computation.6 | async-start | bytes 3981312 | tf_op jit(solution)/shard_map/reduce_scatter | solution.py:326
  1140.1 352.0 %reduce-scatter.11.cloned.1.call-start = ((), (), s32[]{:S(2)}) async-start(), calls=%async_computation.7 | async-start | bytes 3981312 | tf_op jit(solution)/shard_map/reduce_scatter | solution.py:329
  1153.0 237.1 %slice-start = ((s8[7077888]{0:T(1024)(128)(4,1)}), s8[2883584]{0:T(1024)(128)(4,1)S(1)}, s32[]{:S(2)}) async-start(s8[7077888]{0:T(1024)(128)(4,1)} %bitcast.359), calls=%async_computation.11 | async-start | bytes 5767168
  1158.4 367.3 %reduce-scatter.15.cloned.1.call-start = ((), (), s32[]{:S(2)}) async-start(), calls=%async_computation.9 | async-start | bytes 442368
  1381.8 8.3 slice-start.1
  1381.8 8.7 copy-start.3
  1466.9 92.5 %reduce-scatter.13.cloned.1.call-start = ((), (), s32[]{:S(2)}) async-start(), calls=%async_computation.8 | async-start | bytes 1105920
  1479.8 560.0 %all-reduce.13.cloned.1.call-start = ((), (), s32[]{:S(2)}) async-start(), calls=%async_computation.10 | async-start | bytes 28311552 | tf_op jit(solution)/shard_map/psum | solution.py:49
  1487.6 7.1 copy-start.23
  1487.6 552.2 %copy-start.15 = (f32[2304]{0:T(1024)S(1)}, f32[2304]{0:T(1024)}, u32[]{:S(2)}) copy-start(f32[2304]{0:T(1024)} %copy-done.14) | copy-start | bytes 27652
  1487.6 552.2 %copy-start.19 = (f32[2304]{0:T(1024)S(1)}, f32[2304]{0:T(1024)}, u32[]{:S(2)}) copy-start(f32[2304]{0:T(1024)} %copy-done.18) | copy-start | bytes 27652
  1487.7 552.1 %copy-start.27 = (f32[768]{0:T(1024)S(1)}, f32[768]{0:T(1024)}, u32[]{:S(2)}) copy-start(f32[768]{0:T(1024)} %param.36) | copy-start | bytes 9220
  2039.8 48.3 %copy-start.25 = (f32[768]{0:T(1024)S(1)}, f32[768]{0:T(1024)}, u32[]{:S(2)}) copy-start(f32[768]{0:T(1024)} %param.41) | copy-start | bytes 9220
  (15 other events, 39.7 us)
Sparse Core Ops, SparseCore 0:
  60.2 251.0 all-reduce.8
  1134.5 247.2 all-reduce.10
  1385.3 46.9 reduce-scatter.8
  1435.7 48.0 reduce-scatter.10
  1486.7 33.8 reduce-scatter.14
  1523.6 35.7 reduce-scatter.12
  1562.2 477.5 all-reduce.12
where the time goes:
time: 2130 us; the launch traced here: 2110 us
  waiting for transfers between devices  956 us (45%)
  matrix products  450 us (21%)
  local copies, waits for them, and re-layouts  346 us (16%)
  other arithmetic  184 us (9%)
  loops' own time  94.3 us (4%)
  blocking collectives  64.2 us (3%)
    psum x3, waiting for transfers between devices, total_rows(): return lax.psum(values, 'tensor')  924 us
    another operation x50, local copies, waits for them, and re-layouts  126 us
    dot_general x20, matrix products, expert_back(): jnp.einsum('rd,rf->df', block_in, grad_pre, preferred_element_type=jnp.fl...  86.5 us
    scatter-add x40, local copies, waits for them, and re-layouts, expert_back(): acc_down.at[expert_id]  72.3 us
    dot_general x20, matrix products, expert_back(): jnp.einsum('rf,rd->fd', act_out, grad_block, preferred_element_type=jnp.f...  71.4 us
    dot_general x20, matrix products, expert_block(): block_out = jnp.dot(act_out, down_mat, preferred_element_type=jnp.float32)  62.2 us
    dot_general x20, matrix products, expert_back(): jnp.einsum('rd,fd->rf', grad_block, down_mat, preferred_element_type=jnp....  52.5 us
    dot_general x20, matrix products, expert_back(): jnp.einsum('rf,df->rd', grad_pre, up_mat, preferred_element_type=jnp.floa...  51.5 us
  transfers between devices with their start and end apart: 7, of which 4 were waited for; matrix products, arithmetic and copies ran while one was open for 8% of the time, Pallas kernels for 0%

commit v1 on v0

--- a/solution.py
+++ b/solution.py
@@ -46,7 +46,7 @@
 
 
 def total_rows(values):
-    return lax.psum(values, "tensor")
+    return jnp.sum(lax.all_gather(values, "tensor"), axis=0)
 
 
 def group_slots(onehot_int, row_count):

time: 2130 us -> 3080 us (1.45)
  waiting for transfers between devices: 956 us -> 1850 us
  other arithmetic: 184 us -> 243 us
    all_gather x0 -> x4, waiting for transfers between devices: none -> 1800 us  [total_rows(): return jnp.sum(lax.all_gather(values, 'tensor'), axis=0)]
    psum x3 -> x0, waiting for transfers between devices: 924 us -> none  [total_rows(): return lax.psum(values, 'tensor')]
    reduce_sum x0 -> x4, other arithmetic: none -> 55.6 us  [total_rows(): return jnp.sum(lax.all_gather(values, 'tensor'), axis=0)]
  transfers between devices with their start and end apart: 7 -> 8, of which waited for: 4 -> 6; matrix products, arithmetic and copies ran while one was open for 8% -> 7% of each run, Pallas kernels for 0% -> 0%
where the time goes in v1:
time: 3080 us; the launch traced here: 3060 us
  waiting for transfers between devices  1850 us (60%)
  matrix products  453 us (15%)
  local copies, waits for them, and re-layouts  351 us (11%)
  other arithmetic  243 us (8%)
  loops' own time  83.8 us (3%)
  blocking collectives  65.9 us (2%)
    all_gather x4, waiting for transfers between devices, total_rows(): return jnp.sum(lax.all_gather(values, 'tensor'), axis=0)  1800 us
    another operation x50, local copies, waits for them, and re-layouts  126 us
    dot_general x20, matrix products, expert_back(): jnp.einsum('rd,rf->df', block_in, grad_pre, preferred_element_type=jnp.fl...  88 us
    scatter-add x40, local copies, waits for them, and re-layouts, expert_back(): acc_down.at[expert_id]  72.9 us
    dot_general x20, matrix products, expert_back(): jnp.einsum('rf,rd->fd', act_out, grad_block, preferred_element_type=jnp.f...  72.2 us
    dot_general x20, matrix products, expert_block(): block_out = jnp.dot(act_out, down_mat, preferred_element_type=jnp.float32)  62.2 us
  transfers between devices with their start and end apart: 8, of which 6 were waited for; matrix products, arithmetic and copies ran while one was open for 7% of the time, Pallas kernels for 0%

profile of v1, /device:TPU:0, one launch (start us, length us, event | category | flops | bytes accessed | tf_op | source)
XLA Modules:
  0.0 3060.7 jit_solution(8714686938573068212)
XLA Ops:
  13.2 5.2 fusion.82
  28.9 26.4 while.59
  68.3 9.0 scatter_custom_fusion
  77.3 13.6 gather_fusion.2
  91.9 449.2 %all-gather.9.cloned.1.call-done = f32[9216,768]{1,0:T(8,128)} async-done(((f32[2304,768]{1,0:T(8,128)}), f32[9216,768]{1,0:T(8,128)}) %all-gather.9.cloned.1.call-update) | async-done | bytes 28311568 | tf_op jit(solution)/shard_map/all_gather | solution.py:49
  541.1 13.6 reduce_sum.211
  554.7 5.2 fusion.127
  564.2 15.5 add_convert_fusion.2
  581.8 12.8 gather_fusion
  602.5 207.9 %while.60 = (s32[]{:T(128)}, f32[20,128,768]{2,1,0:T(8,128)}, bf16[20,128,768]{2,1,0:T(8,128)(2,1)}, f32[20,128,768]{2,1,0:T(8,128)}, bf16[20,128,768]{2,1,0:T(8...) while((s32[]{:T(128)}, f32[20,128,768]{2,1,0:T(8,128)}, ...), condition=%wide.region_17.18_spmd, body=%wide.region_16.17_spmd.sunk | while | flops 314867712 | bytes 4730031 | solution.py:217
  821.3 537.9 %while.61 = (s32[]{:T(128)}, f32[3,768,768]{2,1,0:T(8,128)}, f32[3,768,768]{1,2,0:T(8,128)}, f32[3,768]{1,0:T(4,128)S(1)}, f32[20,128,768]{2,1,0:T(8,128)}, /*in...) while((s32[]{:T(128)}, f32[3,768,768]{2,1,0:T(8,128)}, ...), condition=%wide.region_23.24_spmd, body=%wide.region_19.23_spmd.sunk | while | flops 613614336 | bytes 32858372 | solution.py:252
  896.1 4.4 fusion.210
  949.9 4.4 fusion.210
  1359.2 12.7 gather_fusion.3
  1372.0 5.2 convert_element_type.143
  1377.3 7.3 convert_element_type.145
  1384.7 13.6 gather_fusion.1
  1398.3 448.1 %all-gather.13.cloned.1.call-done = f32[9216,768]{1,0:T(8,128)} async-done(((f32[2304,768]{1,0:T(8,128)}), f32[9216,768]{1,0:T(8,128)}) %all-gather.13.cloned.1.call-update) | async-done | bytes 28311568 | tf_op jit(solution)/shard_map/all_gather | solution.py:49
  1846.5 14.5 reduce_sum.219
  1861.1 7.0 fusion.128
  1869.2 9.7 fusion.129
  1881.7 51.2 %while.62 = (s32[]{:T(128)}, bf16[3,768,192]{1,2,0:T(8,128)(2,1)S(1)}, bf16[3,768,192]{1,2,0:T(8,128)(2,1)}, bf16[3,768,192]{1,2,0:T(8,128)(2,1)S(1)}, bf16[3,76...) while((s32[]{:T(128)}, ...), condition=%wide.region_29.30_spmd, body=%wide.region_27.29_spmd.sunk | while | flops 1161510144 | bytes 62592684 | solution.py:272
  1975.7 26.1 all-reduce.3
  2002.3 423.0 %all-gather.11.cloned.1.call-done = f32[9216,768]{1,0:T(8,128)} async-done(((f32[2304,768]{1,0:T(8,128)}), f32[9216,768]{1,0:T(8,128)}) %all-gather.11.cloned.1.call-update) | async-done | bytes 28311568 | tf_op jit(solution)/shard_map/all_gather | solution.py:49
  2425.4 13.8 reduce_sum.218
  2446.0 14.4 reduce-scatter.15.cloned.1.call-done
  2461.9 37.4 %reduce-scatter.13.cloned.1.call-done = bf16[96,576]{1,0:T(8,128)(2,1)} async-done(((bf16[768,576]{1,0:T(8,128)(2,1)}), bf16[96,576]{1,0:T(8,128)(2,1)}) %reduce-scatter.13.cloned.1.call-update) | async-done | bytes 110608
  2501.4 475.7 %all-gather.15.cloned.1.call-done = f32[9216,768]{1,0:T(8,128)} async-done(((f32[2304,768]{1,0:T(8,128)}), f32[9216,768]{1,0:T(8,128)}) %all-gather.15.cloned.1.call-update) | async-done | bytes 28311568 | tf_op jit(solution)/shard_map/all_gather | solution.py:49
  2977.1 13.7 reduce_sum.222
  2990.8 5.5 multiply_reduce_fusion.4
  2998.5 39.9 %all-reduce.2 = (f32[768]{0:T(1024)}, f32[768]{0:T(1024)}, f32[768]{0:T(1024)}, f32[3,768]{1,0:T(4,128)}, f32[3,768]{1,0:T(4,128)}, /*index=5*/f32[3,768]{1,0:T(4,128)}) all-reduce(f32[768]{0:T(1024)S(1)} %get-tuple-element.415, f32[768]{0:T(1024)S(1)} %get-tuple-element.414, ...), channel_id=1, replica_groups=mesh['dp'=8,'tensor'=4] {'dp','tensor'}, use_global_device_ids=true, to_apply=%region_34.35 | all-reduce | flops 9216 | bytes 73728 | tf_op jit(solution)/shard_map/psum | solution.py:333
  3038.4 15.1 add_convert_fusion
  (656 shorter events, 846.1 us)
Async XLA Ops:
  7.2 50.9 %copy-start = (bf16[192,768]{1,0:T(8,128)(2,1)S(1)}, bf16[192,768]{1,0:T(8,128)(2,1)}, u32[]{:S(2)}) copy-start(bf16[192,768]{1,0:T(8,128)(2,1)} %param.40) | copy-start | bytes 884740
  7.2 533.9 %all-gather.9.cloned.1.call-start = ((), (), s32[]{:S(2)}) async-start(), calls=%async_computation.6 | async-start | bytes 35389440 | tf_op jit(solution)/shard_map/all_gather | solution.py:49
  9.9 8.5 copy-start.20
  62.1 1784.4 %all-gather.13.cloned.1.call-start = ((), (), s32[]{:S(2)}) async-start(), calls=%async_computation.8 | async-start | bytes 35389440 | tf_op jit(solution)/shard_map/all_gather | solution.py:49
  77.3 13.7 copy-start.45
  77.3 13.7 copy-start.46
  91.1 473.0 %copy-start.34 = (f32[768]{0:T(1024)}, f32[768]{0:T(1024)S(1)}, u32[]{:S(2)}) copy-start(f32[768]{0:T(1024)S(1)} %get-tuple-element.540) | copy-start | bytes 9220
  91.1 473.0 %copy-start.36 = (f32[768]{0:T(1024)}, f32[768]{0:T(1024)S(1)}, u32[]{:S(2)}) copy-start(f32[768]{0:T(1024)S(1)} %get-tuple-element.541) | copy-start | bytes 9220
  91.1 473.0 %copy-start.38 = (f32[768]{0:T(1024)}, f32[768]{0:T(1024)S(1)}, u32[]{:S(2)}) copy-start(f32[768]{0:T(1024)S(1)} %get-tuple-element.542) | copy-start | bytes 9220
  91.8 472.3 %copy-start.14 = (f32[2304]{0:T(1024)}, f32[2304]{0:T(1024)S(1)}, u32[]{:S(2)}) copy-start(f32[2304]{0:T(1024)S(1)} %get-tuple-element.416) | copy-start | bytes 27652
  91.9 472.3 %copy-start.16 = (f32[2304]{0:T(1024)}, f32[2304]{0:T(1024)S(1)}, u32[]{:S(2)}) copy-start(f32[2304]{0:T(1024)S(1)} %get-tuple-element.417) | copy-start | bytes 27652
  91.9 472.3 %copy-start.18 = (f32[2304]{0:T(1024)}, f32[2304]{0:T(1024)S(1)}, u32[]{:S(2)}) copy-start(f32[2304]{0:T(1024)S(1)} %get-tuple-element.418) | copy-start | bytes 27652
  541.1 13.6 copy-start.32
  564.1 15.6 copy-start.30
  1359.2 12.7 copy-start.28
  1372.0 599.1 %reduce-scatter.9.cloned.1.call-start = ((), (), s32[]{:S(2)}) async-start(), calls=%async_computation.4 | async-start | bytes 3981312 | tf_op jit(solution)/shard_map/reduce_scatter | solution.py:326
  1377.3 595.8 %reduce-scatter.11.cloned.1.call-start = ((), (), s32[]{:S(2)}) async-start(), calls=%async_computation.5 | async-start | bytes 3981312 | tf_op jit(solution)/shard_map/reduce_scatter | solution.py:329
  1384.6 1040.7 %all-gather.11.cloned.1.call-start = ((), (), s32[]{:S(2)}) async-start(), calls=%async_computation.7 | async-start | bytes 35389440 | tf_op jit(solution)/shard_map/all_gather | solution.py:49
  1398.3 1062.0 %reduce-scatter.15.cloned.1.call-start = ((), (), s32[]{:S(2)}) async-start(), calls=%async_computation.11 | async-start | bytes 442368
  1846.5 14.5 copy-start.15
  1846.5 14.5 copy-start.17
  1846.5 14.5 copy-start.19
  1846.5 14.5 copy-start.35
  1846.5 14.5 copy-start.37
  1846.5 14.5 copy-start.39
  1861.1 8.2 copy-start.4
  1947.0 552.2 %reduce-scatter.13.cloned.1.call-start = ((), (), s32[]{:S(2)}) async-start(), calls=%async_computation.10 | async-start | bytes 1105920
  1960.0 1017.1 %all-gather.15.cloned.1.call-start = ((), (), s32[]{:S(2)}) async-start(), calls=%async_computation.9 | async-start | bytes 35389440 | tf_op jit(solution)/shard_map/all_gather | solution.py:49
  2977.1 13.7 copy-start.21
  2977.1 13.7 copy-start.25
  2977.1 13.7 copy-start.41
  2990.8 47.6 %copy-start.33 = (f32[768]{0:T(1024)S(1)}, f32[768]{0:T(1024)}, u32[]{:S(2)}) copy-start(f32[768]{0:T(1024)} %param.41) | copy-start | bytes 9220
  (28 other events, 133.7 us)
Sparse Core Ops, SparseCore 0:
  62.2 478.8 all-gather.8
  1372.1 474.3 all-gather.12
  1850.0 46.2 reduce-scatter.8
  1899.7 48.0 reduce-scatter.10
  1949.2 476.1 all-gather.10
  2428.3 32.0 reduce-scatter.14
  2463.5 35.7 reduce-scatter.12
  2501.0 476.1 all-gather.14
